TPU v7x, 32 devices: a whole 2x2x4 slice. The times are simulated.
32 devices in a mesh: dp: 2 (over core), row: 4 (over y, x), col: 4 (over z).
Axes of the slice: x: 2, y: 2, z: 4, core: 2. Of those that a mesh axis runs over, the one named last changes fastest.
Arguments:
- inputs: bfloat16 [2, 16, 4, 16, 2048], P('dp', 'row', None, None, 'col'), may hold values from -6 to 6
- up_weight: bfloat16 [2048, 4096], P(None, 'col'), may hold values from -0.1875 to 0.1875
- down_weight: bfloat16 [2048, 4096], P(None, 'col'), may hold values from -0.125 to 0.125
- kernel: float32 [125, 4096], P(None, 'col'), may hold values from -0.625 to 0.625
- cotangent: bfloat16 [2, 16, 4, 16, 2048], P('dp', 'row', None, None, 'col'), may hold values from -2 to 2
Outputs:
- block_output: bfloat16 [2, 16, 4, 16, 2048], P('dp', 'row', None, None, 'col')
- input_grad: bfloat16 [2, 16, 4, 16, 2048], P('dp', 'row', None, None, 'col')
- up_grad: bfloat16 [2048, 4096], P(('dp', 'row'), 'col')
- down_grad: bfloat16 [2048, 4096], P(('dp', 'row'), 'col')
- kernel_grad: float32 [125, 4096], P(None, 'col')
All inputs are finite; a program needn't handle non-finite values.
Results may differ from a plain program's by a relative error of at most 0.012.
Values may be sent and summed in bfloat16 or wider, within the bound.
A program may use at most 128 MiB of HBM per device.

v0:
```python
import jax
import jax.numpy as jnp
from jax import lax
from jax.sharding import PartitionSpec as P


def with_halo(shard, sides, width):
    for axis, dim in sides:
        peers, length = (lax.axis_size(axis), shard.shape[dim])
        up = [(i, (i + 1) % peers) for i in range(peers - 1)]
        down = [(j, i) for i, j in up]
        last = lax.slice_in_dim(shard, length - width, length, axis=dim)
        initial = lax.slice_in_dim(shard, 0, width, axis=dim)
        before = lax.ppermute(last, axis, up)
        after = lax.ppermute(initial, axis, down)
        shard = jnp.concatenate([before, shard, after], axis=dim)
    return shard


def depth_margin(field):
    extended = with_halo(field, (("row", 1),), 2)
    return jnp.pad(extended, ((0, 0), (0, 0), (2, 2), (2, 2), (0, 0)))


def stencil_sum(padded, kernel, mirror):
    planes = padded.shape[1] - 4
    tile_x = padded.shape[2] - 4
    tile_y = padded.shape[3] - 4
    result = jnp.zeros(padded.shape[:1] + (planes, tile_x, tile_y, padded.shape[4]), jnp.float32)
    for depth_step in range(5):
        for row_step in range(5):
            for col_step in range(5):
                first_z = depth_step + mirror * (4 - 2 * depth_step)
                first_x = row_step + mirror * (4 - 2 * row_step)
                first_y = col_step + mirror * (4 - 2 * col_step)
                window = padded[
                    :,
                    first_z : first_z + planes,
                    first_x : first_x + tile_x,
                    first_y : first_y + tile_y,
                    :,
                ]
                result = result + kernel[25 * depth_step + 5 * row_step + col_step] * window
    return result


def kernel_terms(padded, grad_field):
    planes = grad_field.shape[1]
    tile_x = grad_field.shape[2]
    tile_y = grad_field.shape[3]
    grad_wide = grad_field.astype(jnp.float32)
    rows_list = []
    for depth_step in range(5):
        for row_step in range(5):
            for col_step in range(5):
                window = padded[
                    :,
                    depth_step : depth_step + planes,
                    row_step : row_step + tile_x,
                    col_step : col_step + tile_y,
                    :,
                ]
                rows_list.append(jnp.sum(window * grad_wide, axis=(0, 1, 2, 3)))
    return jnp.stack(rows_list)


def column_sum(partial_value, field_shape):
    return lax.psum_scatter(
        partial_value.reshape(field_shape).astype(jnp.bfloat16),
        "col",
        scatter_dimension=4,
        tiled=True,
    ).astype(jnp.float32)


def spread_product(left_rows, right_rows):
    return lax.dot_general(
        left_rows, right_rows, (((0,), (0,)), ((), ())), preferred_element_type=jnp.float32
    )


def on_device(inputs, up_weight, down_weight, kernel, cotangent):
    states, planes, tile_x, tile_y, local_width = inputs.shape
    voxels = states * planes * tile_x * tile_y
    local_hidden = up_weight.shape[1]
    contract_last = (((1,), (1,)), ((), ()))
    input_rows, cotangent_rows = (
        lax.all_gather(inputs, "col", axis=4, tiled=True),
        lax.all_gather(cotangent, "col", axis=4, tiled=True),
    )
    full_width = input_rows.shape[4]
    field_shape = (states, planes, tile_x, tile_y, full_width)
    hidden_shape = (states, planes, tile_x, tile_y, local_hidden)
    flat_inputs = input_rows.reshape(voxels, full_width)
    hidden = jnp.dot(flat_inputs, up_weight, preferred_element_type=jnp.float32).astype(
        jnp.bfloat16
    )
    hidden_pad = depth_margin(hidden.reshape(hidden_shape))
    preact = stencil_sum(hidden_pad, kernel, 0)
    activation = jax.nn.silu(preact).astype(jnp.bfloat16)
    flat_act = activation.reshape(voxels, local_hidden)
    mixed_share = column_sum(
        lax.dot_general(flat_act, down_weight, contract_last, preferred_element_type=jnp.float32),
        field_shape,
    )
    block_output = (inputs.astype(jnp.float32) + mixed_share).astype(jnp.bfloat16)
    flat_cotangent = cotangent_rows.reshape(voxels, full_width)
    act_grad = jnp.dot(flat_cotangent, down_weight, preferred_element_type=jnp.float32).reshape(
        hidden_shape
    )
    logistic = jax.nn.sigmoid(preact)
    preact_grad = (act_grad * logistic * (1.0 + preact * (1.0 - logistic))).astype(jnp.bfloat16)
    grad_pad = depth_margin(preact_grad)
    hidden_grad = stencil_sum(grad_pad, kernel, 1).astype(jnp.bfloat16)
    kernel_grad = lax.psum(
        kernel_terms(hidden_pad, preact_grad).astype(jnp.bfloat16), ("dp", "row")
    ).astype(jnp.float32)
    flat_grad_hidden = hidden_grad.reshape(voxels, local_hidden)
    input_share = column_sum(
        lax.dot_general(
            flat_grad_hidden, up_weight, contract_last, preferred_element_type=jnp.float32
        ),
        field_shape,
    )
    input_grad = (cotangent.astype(jnp.float32) + input_share).astype(jnp.bfloat16)
    both_share = lax.psum_scatter(
        jnp.concatenate(
            [
                spread_product(flat_inputs, flat_grad_hidden),
                spread_product(flat_cotangent, flat_act),
            ],
            axis=1,
        ).astype(jnp.bfloat16),
        ("dp", "row"),
        scatter_dimension=0,
        tiled=True,
    ).astype(jnp.float32)
    up_share = both_share[:, :local_hidden]
    down_share = both_share[:, local_hidden:]
    up_grad = up_share.astype(jnp.bfloat16)
    down_grad = down_share.astype(jnp.bfloat16)
    return (block_output, input_grad, up_grad, down_grad, kernel_grad)


def solution(mesh):
    placed = (
        P("dp", "row", None, None, "col"),
        P(None, "col"),
        P(None, "col"),
        P(None, "col"),
        P("dp", "row", None, None, "col"),
    )
    return jax.shard_map(
        on_device,
        mesh=mesh,
        in_specs=placed,
        out_specs=(
            P("dp", "row", None, None, "col"),
            P("dp", "row", None, None, "col"),
            P(("dp", "row"), "col"),
            P(("dp", "row"), "col"),
            P(None, "col"),
        ),
        check_vma=False,
    )
```

profile of v0, /device:TPU:0, one launch (start us, length us, event | category | flops | bytes accessed | tf_op | source)
XLA Modules:
  0.0 385.0 jit_solution(17823461748566457241)
XLA Ops:
  7.9 0.7 all-gather.5.cloned.1.call-update
  8.7 1.3 fusion.328
  10.0 2.0 fusion.327
  12.0 1.9 fusion.326
  13.9 1.9 fusion.325
  15.9 2.0 fusion.324
  17.9 22.3 %all-gather.3.cloned.1.call-done = bf16[1,4,4,16,2048]{4,3,2,1,0:T(8,128)(2,1)} async-done(((bf16[1,4,4,16,512]{4,3,2,1,0:T(8,128)(2,1)}), bf16[1,4,4,16,2048]{4,3,2,1,0:T(8,128)(2,1)}) %all-gather.3.cloned.1.call-update) | async-done | bytes 1048592 | tf_op jit(solution)/shard_map/all_gather | solution.py:88
  40.2 3.8 convolution_convert_fusion
  44.5 1.3 collective-permute-start.1
  45.8 4.7 %collective-permute-start = (bf16[1,2,4,16,1024]{4,3,2,1,0:T(8,128)(2,1)S(1)}, bf16[1,2,4,16,1024]{4,3,2,1,0:T(8,128)(2,1)S(1)}, u32[]{:S(2)}, u32[]{:S(2)}) collective-permute-start(bf16[1,2,4,16,1024]{4,3,2,1,0:T(8,128)(2,1)S(1)} %get-tuple-element.142), channel_id=1, source_target_pairs={{0,4},{4,8},{8,12},{1,5},{5,9},{9,13},{2,6},{6,10},{10,14},{3,7},{... | collective-permute-start | bytes 786440 | tf_op jit(solution)/shard_map/ppermute | solution.py:14
  50.5 1.1 fusion.330
  51.7 1.4 fusion.329
  53.3 2.3 collective-permute-done.1
  55.6 0.8 select_maximum_fusion.2
  57.1 28.9 %fusion.159 = f32[1,4,4,16,1024]{4,3,2,1,0:T(8,128)} fusion(bf16[1,4,4,16,1024]{4,3,2,1,0:T(8,128)(2,1)S(1)} %bitcast.210, f32[1024]{0:T(1024)S(1)} %bitcast.420, f32[1024]{0:T(1024)S(1)} %bitcast.422, f32[1024]{0:T(1024)} %bitcast.366, f32[1024]{0:T(1024)} %bitcast.368, f32[1024]{0:T(1024)} %bitcast.370, f32[1024]{0:T(1024)} %bitcast.372, ...), kind=kLoop, calls=%fused_computation.406 | loop fusion | flops 99090432 | bytes 65523712 | tf_op jit(solution)/shard_map/add | solution.py:43
  86.1 6.9 %fusion.303 = (bf16[1024]{0:T(1024)(128)(2,1)}, bf16[1024]{0:T(1024)(128)(2,1)}, bf16[1024]{0:T(1024)(128)(2,1)}, bf16[1024]{0:T(1024)(128)(2,1)}, bf16[1024]{0:...) fusion(bf16[1,8,8,20,1024]{4,3,2,1,0:T(8,128)(2,1)S(1)} %select, ...), kind=kOutput, calls=%fused_computation.550 | convolution fusion | flops 1086573568 | bytes 13658112 | tf_op jit(solution)/shard_map/dot_general | solution.py:108
  93.1 3.4 fusion.308
  96.5 3.4 fusion.309
  99.9 3.4 fusion.306
  103.3 3.4 fusion.304
  106.7 3.3 fusion.305
  110.0 3.4 fusion.307
  113.8 2.3 fusion.21
  116.0 0.8 stack.622
  121.1 0.7 stack.621
  122.5 0.7 stack.504
  127.2 0.7 stack.528
  129.2 0.7 stack.531
  129.9 0.7 stack.532
  132.6 0.7 stack.536
  135.3 0.7 stack.540
  136.0 0.7 stack.542
  136.7 0.7 stack.543
  138.7 0.7 stack.509
  149.9 0.7 stack.561
  151.9 0.7 stack.564
  153.9 0.7 stack.568
  155.3 0.7 stack.570
  156.6 0.7 stack.572
  157.3 0.7 stack.573
  161.4 0.7 stack.623
  164.0 0.7 stack.600
  165.4 0.7 stack.602
  168.1 0.7 stack.606
  169.4 0.7 stack.608
  173.5 0.7 stack.626
  175.0 10.6 %stack.629 = bf16[125,1024]{1,0:T(8,128)(2,1)} concatenate(bf16[1,1024]{1,0:T(2,128)(2,1)S(1)} %stack.504, bf16[1,1024]{1,0:T(2,128)(2,1)S(1)} %stack.505, bf16[1,1024]{1,0:T(2,128)(2,1)S(1)} %stack.506, bf16[1,1024]{1,0:T(2,128)(2,1)S(1)} %stack.507, bf16[1,1024]{1,0:T(2,128)(2,1)S(1)} %stack.508, bf16[1,1024]{1,0:T(2,128)(2,1)S(1)} %stack.509, bf16[1,1024]{1,0:T(2,128)(2,1)S(1)} %stack.510, ...), dimensions={0} | concatenate | bytes 512000 | tf_op jit(solution)/shard_map/stack | solution.py:64
  185.7 1.3 collective-permute-start.3
  187.0 6.4 %collective-permute-start.2 = (bf16[1,2,4,16,1024]{4,3,2,1,0:T(8,128)(2,1)S(1)}, bf16[1,2,4,16,1024]{4,3,2,1,0:T(8,128)(2,1)S(1)}, u32[]{:S(2)}, u32[]{:S(2)}) collective-permute-start(bf16[1,2,4,16,1024]{4,3,2,1,0:T(8,128)(2,1)S(1)} %get-tuple-element.140), channel_id=1, source_target_pairs={{0,4},{4,8},{8,12},{1,5},{5,9},{9,13},{2,6},{6,10},{10,14},{3,7},{... | collective-permute-start | bytes 786440 | tf_op jit(solution)/shard_map/ppermute | solution.py:14
  193.5 4.5 %fusion.10 = bf16[2048,1024]{0,1:T(8,128)(2,1)} fusion(bf16[1,4,4,16,2048]{4,3,2,1,0:T(8,128)(2,1)} %all-gather.5.cloned.1.call-done, f32[1,4,4,16,1024]{4,3,2,1,0:T(8,128)S(1)} %copy-done.7), kind=kOutput, calls=%fused_computation.143 | convolution fusion | flops 1077149696 | bytes 6291456 | tf_op jit(solution)/shard_map/dot_general | solution.py:77
  198.5 1.1 select_maximum_fusion
  200.0 30.2 %add_convert_fusion = bf16[1,4,4,16,1024]{4,3,2,1,0:T(8,128)(2,1)S(1)} fusion(bf16[1,4,4,16,1024]{4,3,2,1,0:T(8,128)(2,1)S(1)} %copy-done.1, bf16[1,2,4,16,1024]{4,3,2,1,0:T(8,128)(2,1)S(1)} %collective-permute-done.2, bf16[1,2,4,16,1024]{4,3,2,1,0:T(8,128)(2,1)S(1)} %collective-permute-done.3, bf16[1,8,8,20,1024]{4,3,2,1,0:T(8,128)(2,1)S(1)} %select_maximum_fusion, ...), kind=kLoop, calls=%fused_computation.560 | loop fusion | flops 99352576 | bytes 64999424 | tf_op jit(solution)/shard_map/convert_element_type | solution.py:114
  230.2 4.5 %fusion.18 = bf16[1,4,4,16,2048]{4,3,2,1,0:T(8,128)(2,1)} fusion(bf16[2048,1024]{1,0:T(8,128)(2,1)} %param.6, bf16[1,4,4,16,1024]{4,3,2,1,0:T(8,128)(2,1)S(1)} %add_convert_fusion), kind=kOutput, calls=%fused_computation.151 | convolution fusion | flops 1074266112 | bytes 5767168 | tf_op jit(solution)/shard_map/dot_general | solution.py:120
  234.8 4.5 %fusion.9 = bf16[2048,1024]{0,1:T(8,128)(2,1)} fusion(bf16[1,4,4,16,2048]{4,3,2,1,0:T(8,128)(2,1)} %all-gather.3.cloned.1.call-done, bf16[1,4,4,16,1024]{4,3,2,1,0:T(8,128)(2,1)S(1)} %add_convert_fusion), kind=kOutput, calls=%fused_computation.142 | convolution fusion | flops 1075838976 | bytes 5767168 | tf_op jit(solution)/shard_map/dot_general | solution.py:77
  239.3 8.4 %pad_maximum_fusion = bf16[2048,2048]{0,1:T(8,128)(2,1)} fusion(bf16[2048,1024]{0,1:T(8,128)(2,1)} %fusion.10, bf16[2048,1024]{0,1:T(8,128)(2,1)} %fusion.9), kind=kLoop, calls=%fused_computation.130 | loop fusion | flops 16777216 | bytes 16777216 | tf_op jit(solution)/shard_map/concatenate | solution.py:127
  247.7 1.8 convert_element_type.1202
  249.6 23.6 %reduce-scatter.4.cloned.1.call-done = bf16[1,4,4,16,512]{4,3,2,1,0:T(8,128)(2,1)} async-done(((bf16[1,4,4,16,2048]{4,3,2,1,0:T(8,128)(2,1)}), bf16[1,4,4,16,512]{4,3,2,1,0:T(8,128)(2,1)}) %reduce-scatter.4.cloned.1.call-update) | async-done | bytes 262160 | tf_op jit(solution)/shard_map/reduce_scatter | solution.py:68
  273.2 1.7 add_convert_fusion.2
  274.9 26.2 %reduce-scatter.6.cloned.1.call-done = bf16[1,4,4,16,512]{4,3,2,1,0:T(8,128)(2,1)} async-done(((bf16[1,4,4,16,2048]{4,3,2,1,0:T(8,128)(2,1)}), bf16[1,4,4,16,512]{4,3,2,1,0:T(8,128)(2,1)}) %reduce-scatter.6.cloned.1.call-update) | async-done | bytes 262160 | tf_op jit(solution)/shard_map/reduce_scatter | solution.py:68
  301.1 1.7 add_convert_fusion.1
  302.9 71.9 %reduce-scatter.8.cloned.1.call-done = bf16[256,2048]{0,1:T(8,128)(2,1)} async-done(((bf16[2048,2048]{0,1:T(8,128)(2,1)}), bf16[256,2048]{0,1:T(8,128)(2,1)}) %reduce-scatter.8.cloned.1.call-update) | async-done | bytes 1048592 | tf_op jit(solution)/shard_map/reduce_scatter | solution.py:126
  374.8 1.3 fusion.321
  376.1 1.0 copy.11
  377.1 1.0 copy.10
  (433 shorter events, 44.2 us)
Async XLA Ops:
  7.2 33.1 %all-gather.3.cloned.1.call-start = ((), (), s32[]{:S(2)}) async-start(), calls=%async_computation.3 | async-start | bytes 1310720 | tf_op jit(solution)/shard_map/all_gather | solution.py:88
  7.9 78.2 %all-gather.5.cloned.1.call-start = ((), (), s32[]{:S(2)}) async-start(), calls=%async_computation.5 | async-start | bytes 1310720 | tf_op jit(solution)/shard_map/all_gather | solution.py:89
  8.6 239.1 %all-reduce.4.cloned.1.call-start = ((), (), s32[]{:S(2)}) async-start(), calls=%async_computation.8 | async-start | bytes 524288 | tf_op jit(solution)/shard_map/psum | solution.py:115
  44.0 12.7 %copy-start.10 = (f32[1,1024]{1,0:T(1,128)S(1)}, f32[1,1024]{1,0:T(1,128)}, u32[]{:S(2)}) copy-start(f32[1,1024]{1,0:T(1,128)} %get-tuple-element.217) | copy-start | bytes 12292
  44.0 12.7 %copy-start.12 = (f32[1,1024]{1,0:T(1,128)S(1)}, f32[1,1024]{1,0:T(1,128)}, u32[]{:S(2)}) copy-start(f32[1,1024]{1,0:T(1,128)} %get-tuple-element.218) | copy-start | bytes 12292
  44.0 12.7 %copy-start.14 = (f32[1,1024]{1,0:T(1,128)S(1)}, f32[1,1024]{1,0:T(1,128)}, u32[]{:S(2)}) copy-start(f32[1,1024]{1,0:T(1,128)} %get-tuple-element.181) | copy-start | bytes 12292
  44.0 12.7 %copy-start.16 = (f32[1,1024]{1,0:T(1,128)S(1)}, f32[1,1024]{1,0:T(1,128)}, u32[]{:S(2)}) copy-start(f32[1,1024]{1,0:T(1,128)} %get-tuple-element.182) | copy-start | bytes 12292
  44.1 12.7 %copy-start.18 = (f32[1,1024]{1,0:T(1,128)S(1)}, f32[1,1024]{1,0:T(1,128)}, u32[]{:S(2)}) copy-start(f32[1,1024]{1,0:T(1,128)} %get-tuple-element.183) | copy-start | bytes 12292
  44.1 12.7 %copy-start.20 = (f32[1,1024]{1,0:T(1,128)S(1)}, f32[1,1024]{1,0:T(1,128)}, u32[]{:S(2)}) copy-start(f32[1,1024]{1,0:T(1,128)} %get-tuple-element.184) | copy-start | bytes 12292
  44.1 12.7 %copy-start.22 = (f32[1,1024]{1,0:T(1,128)S(1)}, f32[1,1024]{1,0:T(1,128)}, u32[]{:S(2)}) copy-start(f32[1,1024]{1,0:T(1,128)} %get-tuple-element.185) | copy-start | bytes 12292
  44.1 12.7 %copy-start.24 = (f32[1,1024]{1,0:T(1,128)S(1)}, f32[1,1024]{1,0:T(1,128)}, u32[]{:S(2)}) copy-start(f32[1,1024]{1,0:T(1,128)} %get-tuple-element.186) | copy-start | bytes 12292
  44.1 12.7 %copy-start.26 = (f32[1,1024]{1,0:T(1,128)S(1)}, f32[1,1024]{1,0:T(1,128)}, u32[]{:S(2)}) copy-start(f32[1,1024]{1,0:T(1,128)} %get-tuple-element.187) | copy-start | bytes 12292
  44.1 12.7 %copy-start.28 = (f32[1,1024]{1,0:T(1,128)S(1)}, f32[1,1024]{1,0:T(1,128)}, u32[]{:S(2)}) copy-start(f32[1,1024]{1,0:T(1,128)} %get-tuple-element.188) | copy-start | bytes 12292
  44.1 12.7 %copy-start.30 = (f32[1,1024]{1,0:T(1,128)S(1)}, f32[1,1024]{1,0:T(1,128)}, u32[]{:S(2)}) copy-start(f32[1,1024]{1,0:T(1,128)} %get-tuple-element.189) | copy-start | bytes 12292
  44.1 12.7 %copy-start.32 = (f32[1,1024]{1,0:T(1,128)S(1)}, f32[1,1024]{1,0:T(1,128)}, u32[]{:S(2)}) copy-start(f32[1,1024]{1,0:T(1,128)} %get-tuple-element.190) | copy-start | bytes 12292
  44.1 12.7 %copy-start.34 = (f32[1,1024]{1,0:T(1,128)S(1)}, f32[1,1024]{1,0:T(1,128)}, u32[]{:S(2)}) copy-start(f32[1,1024]{1,0:T(1,128)} %get-tuple-element.191) | copy-start | bytes 12292
  44.1 12.7 %copy-start.36 = (f32[1,1024]{1,0:T(1,128)S(1)}, f32[1,1024]{1,0:T(1,128)}, u32[]{:S(2)}) copy-start(f32[1,1024]{1,0:T(1,128)} %get-tuple-element.192) | copy-start | bytes 12292
  44.2 12.7 %copy-start.38 = (f32[1,1024]{1,0:T(1,128)S(1)}, f32[1,1024]{1,0:T(1,128)}, u32[]{:S(2)}) copy-start(f32[1,1024]{1,0:T(1,128)} %get-tuple-element.193) | copy-start | bytes 12292
  44.5 11.1 %collective-permute-start.1 = (bf16[1,2,4,16,1024]{4,3,2,1,0:T(8,128)(2,1)S(1)}, bf16[1,2,4,16,1024]{4,3,2,1,0:T(8,128)(2,1)S(1)}, u32[]{:S(2)}, u32[]{:S(2)}) collective-permute-start(bf16[1,2,4,16,1024]{4,3,2,1,0:T(8,128)(2,1)S(1)} %get-tuple-element.141), channel_id=1, source_target_pairs={{4,0},{8,4},{12,8},{5,1},{9,5},{13,9},{6,2},{10,6},{14,10},{7,3},{... | collective-permute-start | bytes 786440 | tf_op jit(solution)/shard_map/ppermute | solution.py:15
  45.8 9.8 %collective-permute-start = (bf16[1,2,4,16,1024]{4,3,2,1,0:T(8,128)(2,1)S(1)}, bf16[1,2,4,16,1024]{4,3,2,1,0:T(8,128)(2,1)S(1)}, u32[]{:S(2)}, u32[]{:S(2)}) collective-permute-start(bf16[1,2,4,16,1024]{4,3,2,1,0:T(8,128)(2,1)S(1)} %get-tuple-element.142), channel_id=1, source_target_pairs={{0,4},{4,8},{8,12},{1,5},{5,9},{9,13},{2,6},{6,10},{10,14},{3,7},{... | collective-permute-start | bytes 786440 | tf_op jit(solution)/shard_map/ppermute | solution.py:14
  93.1 16.9 %copy-start = (bf16[1,4,4,16,1024]{4,3,2,1,0:T(8,128)(2,1)}, bf16[1,4,4,16,1024]{4,3,2,1,0:T(8,128)(2,1)S(1)}, u32[]{:S(2)}) copy-start(bf16[1,4,4,16,1024]{4,3,2,1,0:T(8,128)(2,1)S(1)} %get-tuple-element.268) | copy-start | bytes 1572868
  113.4 60.1 %copy-start.154 = (bf16[1024]{0:T(1024)(128)(2,1)S(1)}, bf16[1024]{0:T(1024)(128)(2,1)}, u32[]{:S(2)}) copy-start(bf16[1024]{0:T(1024)(128)(2,1)} %get-tuple-element.82) | copy-start | bytes 6148
  113.4 60.8 %copy-start.153 = (bf16[1024]{0:T(1024)(128)(2,1)S(1)}, bf16[1024]{0:T(1024)(128)(2,1)}, u32[]{:S(2)}) copy-start(bf16[1024]{0:T(1024)(128)(2,1)} %get-tuple-element.83) | copy-start | bytes 6148
  113.4 60.8 %copy-start.152 = (bf16[1024]{0:T(1024)(128)(2,1)S(1)}, bf16[1024]{0:T(1024)(128)(2,1)}, u32[]{:S(2)}) copy-start(bf16[1024]{0:T(1024)(128)(2,1)} %get-tuple-element.84) | copy-start | bytes 6148
  113.4 60.8 %copy-start.151 = (bf16[1024]{0:T(1024)(128)(2,1)S(1)}, bf16[1024]{0:T(1024)(128)(2,1)}, u32[]{:S(2)}) copy-start(bf16[1024]{0:T(1024)(128)(2,1)} %get-tuple-element.85) | copy-start | bytes 6148
  113.5 60.8 %copy-start.150 = (bf16[1024]{0:T(1024)(128)(2,1)S(1)}, bf16[1024]{0:T(1024)(128)(2,1)}, u32[]{:S(2)}) copy-start(bf16[1024]{0:T(1024)(128)(2,1)} %get-tuple-element.86) | copy-start | bytes 6148
  113.5 60.8 %copy-start.149 = (bf16[1024]{0:T(1024)(128)(2,1)S(1)}, bf16[1024]{0:T(1024)(128)(2,1)}, u32[]{:S(2)}) copy-start(bf16[1024]{0:T(1024)(128)(2,1)} %get-tuple-element.87) | copy-start | bytes 6148
  113.5 60.8 %copy-start.148 = (bf16[1024]{0:T(1024)(128)(2,1)S(1)}, bf16[1024]{0:T(1024)(128)(2,1)}, u32[]{:S(2)}) copy-start(bf16[1024]{0:T(1024)(128)(2,1)} %get-tuple-element.88) | copy-start | bytes 6148
  113.5 60.9 %copy-start.147 = (bf16[1024]{0:T(1024)(128)(2,1)S(1)}, bf16[1024]{0:T(1024)(128)(2,1)}, u32[]{:S(2)}) copy-start(bf16[1024]{0:T(1024)(128)(2,1)} %get-tuple-element.89) | copy-start | bytes 6148
  113.5 60.9 %copy-start.146 = (bf16[1024]{0:T(1024)(128)(2,1)S(1)}, bf16[1024]{0:T(1024)(128)(2,1)}, u32[]{:S(2)}) copy-start(bf16[1024]{0:T(1024)(128)(2,1)} %get-tuple-element.90) | copy-start | bytes 6148
  113.5 60.9 %copy-start.145 = (bf16[1024]{0:T(1024)(128)(2,1)S(1)}, bf16[1024]{0:T(1024)(128)(2,1)}, u32[]{:S(2)}) copy-start(bf16[1024]{0:T(1024)(128)(2,1)} %get-tuple-element.91) | copy-start | bytes 6148
  113.5 60.9 %copy-start.144 = (bf16[1024]{0:T(1024)(128)(2,1)S(1)}, bf16[1024]{0:T(1024)(128)(2,1)}, u32[]{:S(2)}) copy-start(bf16[1024]{0:T(1024)(128)(2,1)} %get-tuple-element.92) | copy-start | bytes 6148
  113.5 60.9 %copy-start.143 = (bf16[1024]{0:T(1024)(128)(2,1)S(1)}, bf16[1024]{0:T(1024)(128)(2,1)}, u32[]{:S(2)}) copy-start(bf16[1024]{0:T(1024)(128)(2,1)} %get-tuple-element.93) | copy-start | bytes 6148
  113.5 60.9 %copy-start.142 = (bf16[1024]{0:T(1024)(128)(2,1)S(1)}, bf16[1024]{0:T(1024)(128)(2,1)}, u32[]{:S(2)}) copy-start(bf16[1024]{0:T(1024)(128)(2,1)} %get-tuple-element.94) | copy-start | bytes 6148
  113.5 60.9 %copy-start.141 = (bf16[1024]{0:T(1024)(128)(2,1)S(1)}, bf16[1024]{0:T(1024)(128)(2,1)}, u32[]{:S(2)}) copy-start(bf16[1024]{0:T(1024)(128)(2,1)} %get-tuple-element.95) | copy-start | bytes 6148
  113.5 60.9 %copy-start.140 = (bf16[1024]{0:T(1024)(128)(2,1)S(1)}, bf16[1024]{0:T(1024)(128)(2,1)}, u32[]{:S(2)}) copy-start(bf16[1024]{0:T(1024)(128)(2,1)} %get-tuple-element.96) | copy-start | bytes 6148
  113.6 61.0 %copy-start.139 = (bf16[1024]{0:T(1024)(128)(2,1)S(1)}, bf16[1024]{0:T(1024)(128)(2,1)}, u32[]{:S(2)}) copy-start(bf16[1024]{0:T(1024)(128)(2,1)} %get-tuple-element.97) | copy-start | bytes 6148
  113.6 61.0 %copy-start.138 = (bf16[1024]{0:T(1024)(128)(2,1)S(1)}, bf16[1024]{0:T(1024)(128)(2,1)}, u32[]{:S(2)}) copy-start(bf16[1024]{0:T(1024)(128)(2,1)} %get-tuple-element.98) | copy-start | bytes 6148
  113.6 61.0 %copy-start.136 = (bf16[1024]{0:T(1024)(128)(2,1)S(1)}, bf16[1024]{0:T(1024)(128)(2,1)}, u32[]{:S(2)}) copy-start(bf16[1024]{0:T(1024)(128)(2,1)} %get-tuple-element.99) | copy-start | bytes 6148
  113.6 61.0 %copy-start.137 = (bf16[1024]{0:T(1024)(128)(2,1)S(1)}, bf16[1024]{0:T(1024)(128)(2,1)}, u32[]{:S(2)}) copy-start(bf16[1024]{0:T(1024)(128)(2,1)} %get-tuple-element.47) | copy-start | bytes 6148
  113.6 61.0 %copy-start.135 = (bf16[1024]{0:T(1024)(128)(2,1)S(1)}, bf16[1024]{0:T(1024)(128)(2,1)}, u32[]{:S(2)}) copy-start(bf16[1024]{0:T(1024)(128)(2,1)} %get-tuple-element.48) | copy-start | bytes 6148
  113.6 61.0 %copy-start.134 = (bf16[1024]{0:T(1024)(128)(2,1)S(1)}, bf16[1024]{0:T(1024)(128)(2,1)}, u32[]{:S(2)}) copy-start(bf16[1024]{0:T(1024)(128)(2,1)} %get-tuple-element.49) | copy-start | bytes 6148
  113.6 61.0 %copy-start.133 = (bf16[1024]{0:T(1024)(128)(2,1)S(1)}, bf16[1024]{0:T(1024)(128)(2,1)}, u32[]{:S(2)}) copy-start(bf16[1024]{0:T(1024)(128)(2,1)} %get-tuple-element.50) | copy-start | bytes 6148
  113.6 61.0 %copy-start.132 = (bf16[1024]{0:T(1024)(128)(2,1)S(1)}, bf16[1024]{0:T(1024)(128)(2,1)}, u32[]{:S(2)}) copy-start(bf16[1024]{0:T(1024)(128)(2,1)} %get-tuple-element.51) | copy-start | bytes 6148
  113.6 61.1 %copy-start.131 = (bf16[1024]{0:T(1024)(128)(2,1)S(1)}, bf16[1024]{0:T(1024)(128)(2,1)}, u32[]{:S(2)}) copy-start(bf16[1024]{0:T(1024)(128)(2,1)} %get-tuple-element.52) | copy-start | bytes 6148
  113.7 61.1 %copy-start.130 = (bf16[1024]{0:T(1024)(128)(2,1)S(1)}, bf16[1024]{0:T(1024)(128)(2,1)}, u32[]{:S(2)}) copy-start(bf16[1024]{0:T(1024)(128)(2,1)} %get-tuple-element.53) | copy-start | bytes 6148
  113.7 61.1 %copy-start.129 = (bf16[1024]{0:T(1024)(128)(2,1)S(1)}, bf16[1024]{0:T(1024)(128)(2,1)}, u32[]{:S(2)}) copy-start(bf16[1024]{0:T(1024)(128)(2,1)} %get-tuple-element.54) | copy-start | bytes 6148
  113.7 61.1 %copy-start.128 = (bf16[1024]{0:T(1024)(128)(2,1)S(1)}, bf16[1024]{0:T(1024)(128)(2,1)}, u32[]{:S(2)}) copy-start(bf16[1024]{0:T(1024)(128)(2,1)} %get-tuple-element.55) | copy-start | bytes 6148
  113.7 61.1 %copy-start.127 = (bf16[1024]{0:T(1024)(128)(2,1)S(1)}, bf16[1024]{0:T(1024)(128)(2,1)}, u32[]{:S(2)}) copy-start(bf16[1024]{0:T(1024)(128)(2,1)} %get-tuple-element.56) | copy-start | bytes 6148
  113.7 61.1 %copy-start.126 = (bf16[1024]{0:T(1024)(128)(2,1)S(1)}, bf16[1024]{0:T(1024)(128)(2,1)}, u32[]{:S(2)}) copy-start(bf16[1024]{0:T(1024)(128)(2,1)} %get-tuple-element.57) | copy-start | bytes 6148
  113.7 61.1 %copy-start.125 = (bf16[1024]{0:T(1024)(128)(2,1)S(1)}, bf16[1024]{0:T(1024)(128)(2,1)}, u32[]{:S(2)}) copy-start(bf16[1024]{0:T(1024)(128)(2,1)} %get-tuple-element.58) | copy-start | bytes 6148
  113.7 61.2 %copy-start.124 = (bf16[1024]{0:T(1024)(128)(2,1)S(1)}, bf16[1024]{0:T(1024)(128)(2,1)}, u32[]{:S(2)}) copy-start(bf16[1024]{0:T(1024)(128)(2,1)} %get-tuple-element.59) | copy-start | bytes 6148
  113.7 61.2 %copy-start.123 = (bf16[1024]{0:T(1024)(128)(2,1)S(1)}, bf16[1024]{0:T(1024)(128)(2,1)}, u32[]{:S(2)}) copy-start(bf16[1024]{0:T(1024)(128)(2,1)} %get-tuple-element.60) | copy-start | bytes 6148
  113.7 61.2 %copy-start.122 = (bf16[1024]{0:T(1024)(128)(2,1)S(1)}, bf16[1024]{0:T(1024)(128)(2,1)}, u32[]{:S(2)}) copy-start(bf16[1024]{0:T(1024)(128)(2,1)} %get-tuple-element.61) | copy-start | bytes 6148
  113.7 61.2 %copy-start.121 = (bf16[1024]{0:T(1024)(128)(2,1)S(1)}, bf16[1024]{0:T(1024)(128)(2,1)}, u32[]{:S(2)}) copy-start(bf16[1024]{0:T(1024)(128)(2,1)} %get-tuple-element.62) | copy-start | bytes 6148
  113.8 61.2 %copy-start.120 = (bf16[1024]{0:T(1024)(128)(2,1)S(1)}, bf16[1024]{0:T(1024)(128)(2,1)}, u32[]{:S(2)}) copy-start(bf16[1024]{0:T(1024)(128)(2,1)} %get-tuple-element.63) | copy-start | bytes 6148
  116.0 77.5 %copy-start.7 = (f32[1,4,4,16,1024]{4,3,2,1,0:T(8,128)S(1)}, f32[1,4,4,16,1024]{4,3,2,1,0:T(8,128)}, u32[]{:S(2)}) copy-start(f32[1,4,4,16,1024]{4,3,2,1,0:T(8,128)} %fusion.159) | copy-start | bytes 3145732
  185.6 87.5 %reduce-scatter.4.cloned.1.call-start = ((), (), s32[]{:S(2)}) async-start(), calls=%async_computation.4 | async-start | bytes 1310720 | tf_op jit(solution)/shard_map/reduce_scatter | solution.py:68
  185.7 12.7 %collective-permute-start.3 = (bf16[1,2,4,16,1024]{4,3,2,1,0:T(8,128)(2,1)S(1)}, bf16[1,2,4,16,1024]{4,3,2,1,0:T(8,128)(2,1)S(1)}, u32[]{:S(2)}, u32[]{:S(2)}) collective-permute-start(bf16[1,2,4,16,1024]{4,3,2,1,0:T(8,128)(2,1)S(1)} %get-tuple-element.139), channel_id=1, source_target_pairs={{4,0},{8,4},{12,8},{5,1},{9,5},{13,9},{6,2},{10,6},{14,10},{7,3},{... | collective-permute-start | bytes 786440 | tf_op jit(solution)/shard_map/ppermute | solution.py:15
  187.0 11.4 %collective-permute-start.2 = (bf16[1,2,4,16,1024]{4,3,2,1,0:T(8,128)(2,1)S(1)}, bf16[1,2,4,16,1024]{4,3,2,1,0:T(8,128)(2,1)S(1)}, u32[]{:S(2)}, u32[]{:S(2)}) collective-permute-start(bf16[1,2,4,16,1024]{4,3,2,1,0:T(8,128)(2,1)S(1)} %get-tuple-element.140), channel_id=1, source_target_pairs={{0,4},{4,8},{8,12},{1,5},{5,9},{9,13},{2,6},{6,10},{10,14},{3,7},{... | collective-permute-start | bytes 786440 | tf_op jit(solution)/shard_map/ppermute | solution.py:14
  193.5 107.7 %reduce-scatter.6.cloned.1.call-start = ((), (), s32[]{:S(2)}) async-start(), calls=%async_computation.6 | async-start | bytes 1310720 | tf_op jit(solution)/shard_map/reduce_scatter | solution.py:68
  234.8 140.0 %reduce-scatter.8.cloned.1.call-start = ((), (), s32[]{:S(2)}) async-start(), calls=%async_computation.7 | async-start | bytes 9437184 | tf_op jit(solution)/shard_map/reduce_scatter | solution.py:126
  247.7 25.5 %copy-start.8 = (bf16[1,4,4,16,512]{4,3,2,1,0:T(8,128)(2,1)S(1)}, bf16[1,4,4,16,512]{4,3,2,1,0:T(8,128)(2,1)}, u32[]{:S(2)}) copy-start(bf16[1,4,4,16,512]{4,3,2,1,0:T(8,128)(2,1)} %param.5) | copy-start | bytes 786436
  247.7 53.5 %copy-start.9 = (bf16[1,4,4,16,512]{4,3,2,1,0:T(8,128)(2,1)S(1)}, bf16[1,4,4,16,512]{4,3,2,1,0:T(8,128)(2,1)}, u32[]{:S(2)}) copy-start(bf16[1,4,4,16,512]{4,3,2,1,0:T(8,128)(2,1)} %param.9) | copy-start | bytes 786436
  (102 other events, 529.4 us)
Sparse Core Ops, SparseCore 0:
  9.6 30.6 all-gather.2
  41.8 27.4 all-gather.4
  185.8 58.5 all-reduce.3
  246.6 26.5 reduce-scatter.3
  275.3 25.7 reduce-scatter.5
  304.9 69.9 reduce-scatter.7
where the time goes:
time: 388 us; the launch traced here: 385 us
  waiting for transfers between devices  148 us (38%)
  other arithmetic  95.6 us (25%)
  local copies, waits for them, and re-layouts  84.1 us (22%)
  matrix products  26.5 us (7%)
  between operations  16.9 us (4%)
  starting transfers between devices  14 us (4%)
    reduce_scatter x1, waiting for transfers between devices, on_device(): lax.psum_scatter(jnp.concatenate([spread_product(flat_inputs, flat_grad_h...  71.9 us
    another operation x126, local copies, waits for them, and re-layouts, kernel_terms(): return jnp.stack(rows_list)  68.4 us
    reduce_scatter x2, waiting for transfers between devices, column_sum(): lax.psum_scatter(partial_value.reshape(field_shape).astype(jnp.bfloat16),...  49.8 us
    convert_element_type x1, other arithmetic, on_device(): hidden_grad = stencil_sum(grad_pad, kernel, 1).astype(jnp.bfloat16)  30.2 us
    add x1, other arithmetic, stencil_sum(): result = result + kernel[25 * depth_step + 5 * row_step + col_step] * window  28.9 us
    all_gather x1, waiting for transfers between devices, on_device(): lax.all_gather(inputs, 'col', axis=4, tiled=True)  22.3 us
    reduce_sum x7, other arithmetic, kernel_terms(): rows_list.append(jnp.sum(window * grad_wide, axis=(0, 1, 2, 3)))  20.7 us
    slice x7, local copies, waits for them, and re-layouts, stencil_sum(): result = result + kernel[25 * depth_step + 5 * row_step + col_step] * window  11.7 us
  transfers between devices with their start and end apart: 10, of which 5 were waited for; matrix products, arithmetic and copies ran while one was open for 27% of the time, Pallas kernels for 0%

commit v1 on v0

--- a/solution.py
+++ b/solution.py
@@ -2,6 +2,19 @@
 import jax.numpy as jnp
 from jax import lax
 from jax.sharding import PartitionSpec as P
+
+
+def gather_around(shard, axis, dim):
+    ways = lax.axis_size(axis)
+    up = [(d, (d + 1) % ways) for d in range(ways)]
+    down = [(d, (d - 1) % ways) for d in range(ways)]
+    earlier, later = ([shard], [shard])
+    for _ in range(ways // 2):
+        earlier.append(lax.ppermute(earlier[-1], axis, up))
+    for _ in range((ways - 1) // 2):
+        later.append(lax.ppermute(later[-1], axis, down))
+    line = jnp.concatenate([*earlier[::-1], *later[1:]], axis=dim)
+    return jnp.roll(line, (lax.axis_index(axis) - ways // 2) * shard.shape[dim], axis=dim)
 
 
 def with_halo(shard, sides, width):
@@ -85,7 +98,7 @@
     local_hidden = up_weight.shape[1]
     contract_last = (((1,), (1,)), ((), ()))
     input_rows, cotangent_rows = (
-        lax.all_gather(inputs, "col", axis=4, tiled=True),
+        gather_around(inputs, "col", 4),
         lax.all_gather(cotangent, "col", axis=4, tiled=True),
     )
     full_width = input_rows.shape[4]

time: 388 us -> 322 us (0.83)
  local copies, waits for them, and re-layouts: 84.1 us -> 28.1 us
  waiting for transfers between devices: 148 us -> 142 us
    another operation x126, local copies, waits for them, and re-layouts: 68.4 us -> 11.3 us  [kernel_terms(): return jnp.stack(rows_list)]
    all_gather x1 -> x0, waiting for transfers between devices: 22.3 us -> none  [on_device(): lax.all_gather(inputs, 'col', axis=4, tiled=True)]
    ppermute x0 -> x3, waiting for transfers between devices: none -> 15.6 us  [the longest x2 15.6 us: gather_around(): earlier.append(lax.ppermute(earlier[-1], axis, up))]
    ppermute x0 -> x3, starting transfers between devices: none -> 5.17 us  [the longest x2 3.08 us: gather_around(): earlier.append(lax.ppermute(earlier[-1], axis, up))]
  transfers between devices with their start and end apart: 10 -> 12, of which waited for: 5 -> 6; matrix products, arithmetic and copies ran while one was open for 27% -> 33% of each run, Pallas kernels for 0% -> 0%
where the time goes in v1:
time: 322 us; the launch traced here: 321 us
  waiting for transfers between devices  142 us (44%)
  other arithmetic  91.9 us (29%)
  local copies, waits for them, and re-layouts  28.1 us (9%)
  matrix products  24.4 us (8%)
  starting transfers between devices  17.7 us (5%)
  between operations  17 us (5%)
    reduce_scatter x1, waiting for transfers between devices, on_device(): lax.psum_scatter(jnp.concatenate([spread_product(flat_inputs, flat_grad_h...  71.9 us
    reduce_scatter x2, waiting for transfers between devices, column_sum(): lax.psum_scatter(partial_value.reshape(field_shape).astype(jnp.bfloat16),...  52.3 us
    convert_element_type x1, other arithmetic, on_device(): hidden_grad = stencil_sum(grad_pad, kernel, 1).astype(jnp.bfloat16)  30.2 us
    add x1, other arithmetic, stencil_sum(): result = result + kernel[25 * depth_step + 5 * row_step + col_step] * window  28.8 us
    reduce_sum x7, other arithmetic, kernel_terms(): rows_list.append(jnp.sum(window * grad_wide, axis=(0, 1, 2, 3)))  17.2 us
    ppermute x2, waiting for transfers between devices, gather_around(): earlier.append(lax.ppermute(earlier[-1], axis, up))  15.6 us
    slice x7, local copies, waits for them, and re-layouts, stencil_sum(): result = result + kernel[25 * depth_step + 5 * row_step + col_step] * window  11.7 us
    another operation x126, local copies, waits for them, and re-layouts, kernel_terms(): return jnp.stack(rows_list)  11.3 us
  transfers between devices with their start and end apart: 12, of which 6 were waited for; matrix products, arithmetic and copies ran while one was open for 33% of the time, Pallas kernels for 0%

profile of v1, /device:TPU:0, one launch (start us, length us, event | category | flops | bytes accessed | tf_op | source)
XLA Modules:
  0.0 320.7 jit_solution(7414247959728036554)
XLA Ops:
  7.2 0.0 copy-start.8
  7.2 0.0 all-gather.2.cloned.1.call-start
  7.2 3.1 collective-permute-start
  10.3 2.1 collective-permute-start.2
  12.4 0.0 all-gather.2.cloned.1.call-update
  12.4 0.0 all-reduce.4.cloned.1.call-start
  12.5 1.3 fusion.327
  13.8 2.0 fusion.326
  15.8 1.9 fusion.325
  17.7 2.0 collective-permute-done
  19.7 1.9 fusion.324
  21.7 1.4 fusion.323
  23.3 13.6 %collective-permute-done.1 = bf16[1,4,4,16,512]{4,3,2,1,0:T(8,128)(2,1)S(1)} collective-permute-done((bf16[1,4,4,16,512]{4,3,2,1,0:T(8,128)(2,1)S(1)}, bf16[1,4,4,16,512]{4,3,2,1,0:T(8,128)(2,1)S(1)}, u32[]{:S(2)}, u32[]{:S(2)}) %collective-permute-start.1) | collective-permute-done | bytes 262176 | tf_op jit(solution)/shard_map/ppermute | solution.py:13
  37.0 1.0 constant_dynamic-update-slice_fusion.5
  38.1 0.1 constant_dynamic-slice_fusion
  38.2 1.3 convolution_convert_fusion
  39.7 0.0 copy-start.54
  39.8 0.0 copy-start.56
  40.0 1.3 collective-permute-start.4
  41.3 4.7 %collective-permute-start.3 = (bf16[1,2,4,16,1024]{4,3,2,1,0:T(8,128)(2,1)S(1)}, bf16[1,2,4,16,1024]{4,3,2,1,0:T(8,128)(2,1)S(1)}, u32[]{:S(2)}, u32[]{:S(2)}) collective-permute-start(bf16[1,2,4,16,1024]{4,3,2,1,0:T(8,128)(2,1)S(1)} %get-tuple-element.142), channel_id=1, source_target_pairs={{0,4},{4,8},{8,12},{1,5},{5,9},{9,13},{2,6},{6,10},{10,14},{3,7},{... | collective-permute-start | bytes 786440 | tf_op jit(solution)/shard_map/ppermute | solution.py:27
  46.0 1.1 fusion.329
  47.2 2.0 fusion.328
  49.3 1.6 collective-permute-done.4
  51.0 0.8 select_maximum_fusion.2
  52.6 28.8 %fusion.158 = f32[1,4,4,16,1024]{4,3,2,1,0:T(8,128)} fusion(bf16[1,4,4,16,1024]{4,3,2,1,0:T(8,128)(2,1)S(1)} %bitcast.206, f32[1024]{0:T(1024)S(1)} %bitcast.417, f32[1024]{0:T(1024)S(1)} %bitcast.419, f32[1024]{0:T(1024)S(1)} %bitcast.363, f32[1024]{0:T(1024)S(1)} %bitcast.365, f32[1024]{0:T(1024)S(1)} %bitcast.367, f32[1024]{0:T(1024)S(1)} %bitcast.369, ...), kind=kLoop, calls=%fused_computation.405 | loop fusion | flops 99090432 | bytes 65523712 | tf_op jit(solution)/shard_map/add | solution.py:56
  81.4 0.0 all-gather.2.cloned.1.call-done
  81.4 6.3 %fusion.302 = (bf16[1024]{0:T(1024)(128)(2,1)S(1)}, bf16[1024]{0:T(1024)(128)(2,1)S(1)}, bf16[1024]{0:T(1024)(128)(2,1)S(1)}, bf16[1024]{0:T(1024)(128)(2,1)S(1)...) fusion(bf16[1,8,8,20,1024]{4,3,2,1,0:T(8,128)(2,1)S(1)} %select, ...), kind=kOutput, calls=%fused_computation.549 | convolution fusion | flops 1086573568 | bytes 13658112 | tf_op jit(solution)/shard_map/dot_general | solution.py:121
  87.7 0.0 copy-start
  87.8 2.8 fusion.307
  90.5 2.8 fusion.308
  93.4 3.0 fusion.305
  96.4 2.8 fusion.303
  99.2 2.6 fusion.304
  101.8 2.8 fusion.306
  104.7 0.4 fusion.296
  106.7 10.6 %stack.629 = bf16[125,1024]{1,0:T(8,128)(2,1)} concatenate(bf16[1,1024]{1,0:T(2,128)(2,1)S(1)} %stack.504, bf16[1,1024]{1,0:T(2,128)(2,1)S(1)} %stack.505, bf16[1,1024]{1,0:T(2,128)(2,1)S(1)} %stack.506, bf16[1,1024]{1,0:T(2,128)(2,1)S(1)} %stack.507, bf16[1,1024]{1,0:T(2,128)(2,1)S(1)} %stack.508, bf16[1,1024]{1,0:T(2,128)(2,1)S(1)} %stack.509, bf16[1,1024]{1,0:T(2,128)(2,1)S(1)} %stack.510, ...), dimensions={0} | concatenate | bytes 512000 | tf_op jit(solution)/shard_map/stack | solution.py:77
  117.4 0.0 all-reduce.4.cloned.1.call-update
  117.4 0.0 reduce-scatter.4.cloned.1.call-start
  117.4 1.3 collective-permute-start.6
  118.8 5.0 %collective-permute-start.5 = (bf16[1,2,4,16,1024]{4,3,2,1,0:T(8,128)(2,1)S(1)}, bf16[1,2,4,16,1024]{4,3,2,1,0:T(8,128)(2,1)S(1)}, u32[]{:S(2)}, u32[]{:S(2)}) collective-permute-start(bf16[1,2,4,16,1024]{4,3,2,1,0:T(8,128)(2,1)S(1)} %get-tuple-element.140), channel_id=1, source_target_pairs={{0,4},{4,8},{8,12},{1,5},{5,9},{9,13},{2,6},{6,10},{10,14},{3,7},{... | collective-permute-start | bytes 786440 | tf_op jit(solution)/shard_map/ppermute | solution.py:27
  123.8 4.5 %fusion.20 = bf16[1,4,4,16,2048]{4,3,2,1,0:T(8,128)(2,1)} fusion(bf16[2048,1024]{1,0:T(8,128)(2,1)} %param.7, f32[1,4,4,16,1024]{4,3,2,1,0:T(8,128)S(1)} %copy-done.10), kind=kOutput, calls=%fused_computation.151 | convolution fusion | flops 1075576832 | bytes 6291456 | tf_op jit(solution)/shard_map/dot_general | solution.py:116
  128.5 0.0 copy-start.55
  128.5 0.0 copy-start.57
  128.6 0.0 reduce-scatter.4.cloned.1.call-update
  128.7 0.0 reduce-scatter.6.cloned.1.call-start
  128.7 1.1 select_maximum_fusion
  130.3 30.2 %add_convert_fusion = bf16[1,4,4,16,1024]{4,3,2,1,0:T(8,128)(2,1)S(1)} fusion(bf16[1,4,4,16,1024]{4,3,2,1,0:T(8,128)(2,1)S(1)} %copy-done.1, bf16[1,2,4,16,1024]{4,3,2,1,0:T(8,128)(2,1)S(1)} %collective-permute-done.5, bf16[1,2,4,16,1024]{4,3,2,1,0:T(8,128)(2,1)S(1)} %collective-permute-done.6, bf16[1,8,8,20,1024]{4,3,2,1,0:T(8,128)(2,1)S(1)} %select_maximum_fusion, ...), kind=kLoop, calls=%fused_computation.559 | loop fusion | flops 99352576 | bytes 64999424 | tf_op jit(solution)/shard_map/convert_element_type | solution.py:127
  160.5 4.5 %fusion.17 = bf16[1,4,4,16,2048]{4,3,2,1,0:T(8,128)(2,1)} fusion(bf16[2048,1024]{1,0:T(8,128)(2,1)} %param.6, bf16[1,4,4,16,1024]{4,3,2,1,0:T(8,128)(2,1)S(1)} %add_convert_fusion), kind=kOutput, calls=%fused_computation.150 | convolution fusion | flops 1074266112 | bytes 5767168 | tf_op jit(solution)/shard_map/dot_general | solution.py:133
  165.0 0.0 reduce-scatter.6.cloned.1.call-update
  165.0 0.0 reduce-scatter.8.cloned.1.call-start
  165.1 4.6 %fusion.9 = bf16[2048,1024]{0,1:T(8,128)(2,1)} fusion(bf16[1,4,4,16,2048]{4,3,2,1,0:T(8,128)(2,1)} %all-gather.2.cloned.1.call-done, f32[1,4,4,16,1024]{4,3,2,1,0:T(8,128)S(1)} %copy-done.10), kind=kOutput, calls=%fused_computation.142 | convolution fusion | flops 1077149696 | bytes 6291456 | tf_op jit(solution)/shard_map/dot_general | solution.py:90
  169.7 3.3 %bitcast_convert_fusion.1 = bf16[2048,1024]{0,1:T(8,128)(2,1)} fusion(bf16[1,4,4,16,2048]{4,3,2,1,0:T(8,128)(2,1)S(1)} %copy-done.5, bf16[1,4,4,16,1024]{4,3,2,1,0:T(8,128)(2,1)S(1)} %add_convert_fusion), kind=kOutput, calls=%fused_computation.132 | convolution fusion | flops 1075838976 | bytes 5767168 | tf_op jit(solution)/shard_map/dot_general | solution.py:90
  173.0 8.4 %pad_maximum_fusion = bf16[2048,2048]{0,1:T(8,128)(2,1)} fusion(bf16[2048,1024]{0,1:T(8,128)(2,1)} %fusion.9, bf16[2048,1024]{0,1:T(8,128)(2,1)} %bitcast_convert_fusion.1), kind=kLoop, calls=%fused_computation.130 | loop fusion | flops 16777216 | bytes 16777216 | tf_op jit(solution)/shard_map/concatenate | solution.py:140
  181.3 0.0 reduce-scatter.8.cloned.1.call-update
  181.4 0.0 all-reduce.4.cloned.1.call-done
  181.4 1.8 convert_element_type.1202
  183.2 26.0 %reduce-scatter.4.cloned.1.call-done = bf16[1,4,4,16,512]{4,3,2,1,0:T(8,128)(2,1)} async-done(((bf16[1,4,4,16,2048]{4,3,2,1,0:T(8,128)(2,1)}), bf16[1,4,4,16,512]{4,3,2,1,0:T(8,128)(2,1)}) %reduce-scatter.4.cloned.1.call-update) | async-done | bytes 262160 | tf_op jit(solution)/shard_map/reduce_scatter | solution.py:81
  209.2 1.7 add_convert_fusion.2
  211.0 26.3 %reduce-scatter.6.cloned.1.call-done = bf16[1,4,4,16,512]{4,3,2,1,0:T(8,128)(2,1)} async-done(((bf16[1,4,4,16,2048]{4,3,2,1,0:T(8,128)(2,1)}), bf16[1,4,4,16,512]{4,3,2,1,0:T(8,128)(2,1)}) %reduce-scatter.6.cloned.1.call-update) | async-done | bytes 262160 | tf_op jit(solution)/shard_map/reduce_scatter | solution.py:81
  237.3 1.7 add_convert_fusion.1
  239.0 71.9 %reduce-scatter.8.cloned.1.call-done = bf16[256,2048]{0,1:T(8,128)(2,1)} async-done(((bf16[2048,2048]{0,1:T(8,128)(2,1)}), bf16[256,2048]{0,1:T(8,128)(2,1)}) %reduce-scatter.8.cloned.1.call-update) | async-done | bytes 1048592 | tf_op jit(solution)/shard_map/reduce_scatter | solution.py:139
  310.9 1.3 fusion.320
  312.2 1.0 copy.11
  313.2 1.0 copy.10
  (391 shorter events, 1.5 us)
Async XLA Ops:
  7.2 30.9 %copy-start.8 = (bf16[1,4,4,16,512]{4,3,2,1,0:T(8,128)(2,1)S(1)}, bf16[1,4,4,16,512]{4,3,2,1,0:T(8,128)(2,1)}, u32[]{:S(2)}) copy-start(bf16[1,4,4,16,512]{4,3,2,1,0:T(8,128)(2,1)} %param.5) | copy-start | bytes 786436
  7.2 74.2 %all-gather.2.cloned.1.call-start = ((), (), s32[]{:S(2)}) async-start(), calls=%async_computation.4 | async-start | bytes 1310720 | tf_op jit(solution)/shard_map/all_gather | solution.py:102
  7.2 12.5 %collective-permute-start = (bf16[1,4,4,16,512]{4,3,2,1,0:T(8,128)(2,1)}, bf16[1,4,4,16,512]{4,3,2,1,0:T(8,128)(2,1)S(1)}, u32[]{:S(2)}, u32[]{:S(2)}) collective-permute-start(bf16[1,4,4,16,512]{4,3,2,1,0:T(8,128)(2,1)} %param.5), channel_id=1, source_target_pairs={{0,1},{1,2},{2,3},{3,0},{4,5},{5,6},{6,7},{7,4},{8,9},{9,10},{10,1... | collective-permute-start | bytes 786440 | tf_op jit(solution)/shard_map/ppermute | solution.py:13
  10.3 27.6 %collective-permute-start.2 = (bf16[1,4,4,16,512]{4,3,2,1,0:T(8,128)(2,1)}, bf16[1,4,4,16,512]{4,3,2,1,0:T(8,128)(2,1)S(1)}, u32[]{:S(2)}, u32[]{:S(2)}) collective-permute-start(bf16[1,4,4,16,512]{4,3,2,1,0:T(8,128)(2,1)} %param.5), channel_id=1, source_target_pairs={{0,3},{1,0},{2,1},{3,2},{4,7},{5,4},{6,5},{7,6},{8,11},{9,8},{10,9... | collective-permute-start | bytes 786440 | tf_op jit(solution)/shard_map/ppermute | solution.py:15
  12.4 169.0 %all-reduce.4.cloned.1.call-start = ((), (), s32[]{:S(2)}) async-start(), calls=%async_computation.7 | async-start | bytes 524288 | tf_op jit(solution)/shard_map/psum | solution.py:128
  19.7 17.2 %collective-permute-start.1 = (bf16[1,4,4,16,512]{4,3,2,1,0:T(8,128)(2,1)S(1)}, bf16[1,4,4,16,512]{4,3,2,1,0:T(8,128)(2,1)S(1)}, u32[]{:S(2)}, u32[]{:S(2)}) collective-permute-start(bf16[1,4,4,16,512]{4,3,2,1,0:T(8,128)(2,1)S(1)} %collective-permute-done), channel_id=1, source_target_pairs={{0,1},{1,2},{2,3},{3,0},{4,5},{5,6},{6,7},{7,4},{8,9},{9,10},{10,1... | collective-permute-start | bytes 786440 | tf_op jit(solution)/shard_map/ppermute | solution.py:13
  23.1 28.7 %copy-start.91 = (f32[1,1024]{1,0:T(1,128)}, f32[1,1024]{1,0:T(1,128)S(1)}, u32[]{:S(2)}) copy-start(f32[1,1024]{1,0:T(1,128)S(1)} %get-tuple-element.143) | copy-start | bytes 12292
  23.1 28.7 %copy-start.92 = (f32[1,1024]{1,0:T(1,128)}, f32[1,1024]{1,0:T(1,128)S(1)}, u32[]{:S(2)}) copy-start(f32[1,1024]{1,0:T(1,128)S(1)} %get-tuple-element.144) | copy-start | bytes 12292
  23.1 28.7 %copy-start.93 = (f32[1,1024]{1,0:T(1,128)}, f32[1,1024]{1,0:T(1,128)S(1)}, u32[]{:S(2)}) copy-start(f32[1,1024]{1,0:T(1,128)S(1)} %get-tuple-element.145) | copy-start | bytes 12292
  23.1 28.7 %copy-start.94 = (f32[1,1024]{1,0:T(1,128)}, f32[1,1024]{1,0:T(1,128)S(1)}, u32[]{:S(2)}) copy-start(f32[1,1024]{1,0:T(1,128)S(1)} %get-tuple-element.146) | copy-start | bytes 12292
  23.1 28.7 %copy-start.95 = (f32[1,1024]{1,0:T(1,128)}, f32[1,1024]{1,0:T(1,128)S(1)}, u32[]{:S(2)}) copy-start(f32[1,1024]{1,0:T(1,128)S(1)} %get-tuple-element.147) | copy-start | bytes 12292
  23.2 28.7 %copy-start.96 = (f32[1,1024]{1,0:T(1,128)}, f32[1,1024]{1,0:T(1,128)S(1)}, u32[]{:S(2)}) copy-start(f32[1,1024]{1,0:T(1,128)S(1)} %get-tuple-element.148) | copy-start | bytes 12292
  23.2 28.7 %copy-start.97 = (f32[1,1024]{1,0:T(1,128)}, f32[1,1024]{1,0:T(1,128)S(1)}, u32[]{:S(2)}) copy-start(f32[1,1024]{1,0:T(1,128)S(1)} %get-tuple-element.149) | copy-start | bytes 12292
  23.2 28.7 %copy-start.98 = (f32[1,1024]{1,0:T(1,128)}, f32[1,1024]{1,0:T(1,128)S(1)}, u32[]{:S(2)}) copy-start(f32[1,1024]{1,0:T(1,128)S(1)} %get-tuple-element.150) | copy-start | bytes 12292
  23.2 28.7 %copy-start.99 = (f32[1,1024]{1,0:T(1,128)}, f32[1,1024]{1,0:T(1,128)S(1)}, u32[]{:S(2)}) copy-start(f32[1,1024]{1,0:T(1,128)S(1)} %get-tuple-element.151) | copy-start | bytes 12292
  23.2 28.7 %copy-start.100 = (f32[1,1024]{1,0:T(1,128)}, f32[1,1024]{1,0:T(1,128)S(1)}, u32[]{:S(2)}) copy-start(f32[1,1024]{1,0:T(1,128)S(1)} %get-tuple-element.152) | copy-start | bytes 12292
  23.2 28.7 %copy-start.101 = (f32[1,1024]{1,0:T(1,128)}, f32[1,1024]{1,0:T(1,128)S(1)}, u32[]{:S(2)}) copy-start(f32[1,1024]{1,0:T(1,128)S(1)} %get-tuple-element.153) | copy-start | bytes 12292
  23.2 28.7 %copy-start.102 = (f32[1,1024]{1,0:T(1,128)}, f32[1,1024]{1,0:T(1,128)S(1)}, u32[]{:S(2)}) copy-start(f32[1,1024]{1,0:T(1,128)S(1)} %get-tuple-element.154) | copy-start | bytes 12292
  23.2 28.7 %copy-start.103 = (f32[1,1024]{1,0:T(1,128)}, f32[1,1024]{1,0:T(1,128)S(1)}, u32[]{:S(2)}) copy-start(f32[1,1024]{1,0:T(1,128)S(1)} %get-tuple-element.155) | copy-start | bytes 12292
  23.2 28.7 %copy-start.104 = (f32[1,1024]{1,0:T(1,128)}, f32[1,1024]{1,0:T(1,128)S(1)}, u32[]{:S(2)}) copy-start(f32[1,1024]{1,0:T(1,128)S(1)} %get-tuple-element.156) | copy-start | bytes 12292
  23.2 28.7 %copy-start.105 = (f32[1,1024]{1,0:T(1,128)}, f32[1,1024]{1,0:T(1,128)S(1)}, u32[]{:S(2)}) copy-start(f32[1,1024]{1,0:T(1,128)S(1)} %get-tuple-element.157) | copy-start | bytes 12292
  23.3 28.7 %copy-start.106 = (f32[1,1024]{1,0:T(1,128)}, f32[1,1024]{1,0:T(1,128)S(1)}, u32[]{:S(2)}) copy-start(f32[1,1024]{1,0:T(1,128)S(1)} %get-tuple-element.158) | copy-start | bytes 12292
  23.3 28.7 %copy-start.107 = (f32[1,1024]{1,0:T(1,128)}, f32[1,1024]{1,0:T(1,128)S(1)}, u32[]{:S(2)}) copy-start(f32[1,1024]{1,0:T(1,128)S(1)} %get-tuple-element.159) | copy-start | bytes 12292
  23.3 28.7 %copy-start.108 = (f32[1,1024]{1,0:T(1,128)}, f32[1,1024]{1,0:T(1,128)S(1)}, u32[]{:S(2)}) copy-start(f32[1,1024]{1,0:T(1,128)S(1)} %get-tuple-element.160) | copy-start | bytes 12292
  23.3 28.7 %copy-start.109 = (f32[1,1024]{1,0:T(1,128)}, f32[1,1024]{1,0:T(1,128)S(1)}, u32[]{:S(2)}) copy-start(f32[1,1024]{1,0:T(1,128)S(1)} %get-tuple-element.161) | copy-start | bytes 12292
  23.3 14.9 %copy-start.128 = (bf16[2048,1024]{1,0:T(8,128)(2,1)S(1)}, bf16[2048,1024]{1,0:T(8,128)(2,1)}, u32[]{:S(2)}) copy-start(bf16[2048,1024]{1,0:T(8,128)(2,1)} %param.6) | copy-start | bytes 12582916
  39.5 12.7 %copy-start.12 = (f32[1,1024]{1,0:T(1,128)S(1)}, f32[1,1024]{1,0:T(1,128)}, u32[]{:S(2)}) copy-start(f32[1,1024]{1,0:T(1,128)} %get-tuple-element.217) | copy-start | bytes 12292
  39.5 12.7 %copy-start.14 = (f32[1,1024]{1,0:T(1,128)S(1)}, f32[1,1024]{1,0:T(1,128)}, u32[]{:S(2)}) copy-start(f32[1,1024]{1,0:T(1,128)} %get-tuple-element.218) | copy-start | bytes 12292
  39.6 12.7 %copy-start.16 = (f32[1,1024]{1,0:T(1,128)S(1)}, f32[1,1024]{1,0:T(1,128)}, u32[]{:S(2)}) copy-start(f32[1,1024]{1,0:T(1,128)} %get-tuple-element.181) | copy-start | bytes 12292
  39.6 12.7 %copy-start.18 = (f32[1,1024]{1,0:T(1,128)S(1)}, f32[1,1024]{1,0:T(1,128)}, u32[]{:S(2)}) copy-start(f32[1,1024]{1,0:T(1,128)} %get-tuple-element.182) | copy-start | bytes 12292
  39.6 12.7 %copy-start.20 = (f32[1,1024]{1,0:T(1,128)S(1)}, f32[1,1024]{1,0:T(1,128)}, u32[]{:S(2)}) copy-start(f32[1,1024]{1,0:T(1,128)} %get-tuple-element.183) | copy-start | bytes 12292
  39.6 12.7 %copy-start.22 = (f32[1,1024]{1,0:T(1,128)S(1)}, f32[1,1024]{1,0:T(1,128)}, u32[]{:S(2)}) copy-start(f32[1,1024]{1,0:T(1,128)} %get-tuple-element.184) | copy-start | bytes 12292
  39.6 12.7 %copy-start.24 = (f32[1,1024]{1,0:T(1,128)S(1)}, f32[1,1024]{1,0:T(1,128)}, u32[]{:S(2)}) copy-start(f32[1,1024]{1,0:T(1,128)} %get-tuple-element.185) | copy-start | bytes 12292
  39.6 12.7 %copy-start.26 = (f32[1,1024]{1,0:T(1,128)S(1)}, f32[1,1024]{1,0:T(1,128)}, u32[]{:S(2)}) copy-start(f32[1,1024]{1,0:T(1,128)} %get-tuple-element.186) | copy-start | bytes 12292
  39.6 12.7 %copy-start.28 = (f32[1,1024]{1,0:T(1,128)S(1)}, f32[1,1024]{1,0:T(1,128)}, u32[]{:S(2)}) copy-start(f32[1,1024]{1,0:T(1,128)} %get-tuple-element.187) | copy-start | bytes 12292
  39.6 12.7 %copy-start.30 = (f32[1,1024]{1,0:T(1,128)S(1)}, f32[1,1024]{1,0:T(1,128)}, u32[]{:S(2)}) copy-start(f32[1,1024]{1,0:T(1,128)} %get-tuple-element.188) | copy-start | bytes 12292
  39.6 12.7 %copy-start.32 = (f32[1,1024]{1,0:T(1,128)S(1)}, f32[1,1024]{1,0:T(1,128)}, u32[]{:S(2)}) copy-start(f32[1,1024]{1,0:T(1,128)} %get-tuple-element.189) | copy-start | bytes 12292
  39.6 12.7 %copy-start.34 = (f32[1,1024]{1,0:T(1,128)S(1)}, f32[1,1024]{1,0:T(1,128)}, u32[]{:S(2)}) copy-start(f32[1,1024]{1,0:T(1,128)} %get-tuple-element.190) | copy-start | bytes 12292
  39.7 12.7 %copy-start.36 = (f32[1,1024]{1,0:T(1,128)S(1)}, f32[1,1024]{1,0:T(1,128)}, u32[]{:S(2)}) copy-start(f32[1,1024]{1,0:T(1,128)} %get-tuple-element.191) | copy-start | bytes 12292
  39.7 12.7 %copy-start.38 = (f32[1,1024]{1,0:T(1,128)S(1)}, f32[1,1024]{1,0:T(1,128)}, u32[]{:S(2)}) copy-start(f32[1,1024]{1,0:T(1,128)} %get-tuple-element.192) | copy-start | bytes 12292
  39.7 12.7 %copy-start.40 = (f32[1,1024]{1,0:T(1,128)S(1)}, f32[1,1024]{1,0:T(1,128)}, u32[]{:S(2)}) copy-start(f32[1,1024]{1,0:T(1,128)} %get-tuple-element.193) | copy-start | bytes 12292
  39.7 12.7 %copy-start.42 = (f32[1,1024]{1,0:T(1,128)S(1)}, f32[1,1024]{1,0:T(1,128)}, u32[]{:S(2)}) copy-start(f32[1,1024]{1,0:T(1,128)} %get-tuple-element.194) | copy-start | bytes 12292
  39.7 12.7 %copy-start.44 = (f32[1,1024]{1,0:T(1,128)S(1)}, f32[1,1024]{1,0:T(1,128)}, u32[]{:S(2)}) copy-start(f32[1,1024]{1,0:T(1,128)} %get-tuple-element.195) | copy-start | bytes 12292
  39.7 12.7 %copy-start.46 = (f32[1,1024]{1,0:T(1,128)S(1)}, f32[1,1024]{1,0:T(1,128)}, u32[]{:S(2)}) copy-start(f32[1,1024]{1,0:T(1,128)} %get-tuple-element.196) | copy-start | bytes 12292
  39.7 12.7 %copy-start.48 = (f32[1,1024]{1,0:T(1,128)S(1)}, f32[1,1024]{1,0:T(1,128)}, u32[]{:S(2)}) copy-start(f32[1,1024]{1,0:T(1,128)} %get-tuple-element.197) | copy-start | bytes 12292
  39.7 12.7 %copy-start.50 = (f32[1,1024]{1,0:T(1,128)S(1)}, f32[1,1024]{1,0:T(1,128)}, u32[]{:S(2)}) copy-start(f32[1,1024]{1,0:T(1,128)} %get-tuple-element.198) | copy-start | bytes 12292
  39.7 12.7 %copy-start.52 = (f32[1,1024]{1,0:T(1,128)S(1)}, f32[1,1024]{1,0:T(1,128)}, u32[]{:S(2)}) copy-start(f32[1,1024]{1,0:T(1,128)} %get-tuple-element.199) | copy-start | bytes 12292
  39.7 12.7 %copy-start.54 = (f32[1,1024]{1,0:T(1,128)S(1)}, f32[1,1024]{1,0:T(1,128)}, u32[]{:S(2)}) copy-start(f32[1,1024]{1,0:T(1,128)} %get-tuple-element.162) | copy-start | bytes 12292
  39.8 12.7 %copy-start.56 = (f32[1,1024]{1,0:T(1,128)S(1)}, f32[1,1024]{1,0:T(1,128)}, u32[]{:S(2)}) copy-start(f32[1,1024]{1,0:T(1,128)} %get-tuple-element.163) | copy-start | bytes 12292
  39.8 12.7 %copy-start.58 = (f32[1,1024]{1,0:T(1,128)S(1)}, f32[1,1024]{1,0:T(1,128)}, u32[]{:S(2)}) copy-start(f32[1,1024]{1,0:T(1,128)} %get-tuple-element.164) | copy-start | bytes 12292
  39.8 12.7 %copy-start.60 = (f32[1,1024]{1,0:T(1,128)S(1)}, f32[1,1024]{1,0:T(1,128)}, u32[]{:S(2)}) copy-start(f32[1,1024]{1,0:T(1,128)} %get-tuple-element.165) | copy-start | bytes 12292
  39.8 12.7 %copy-start.62 = (f32[1,1024]{1,0:T(1,128)S(1)}, f32[1,1024]{1,0:T(1,128)}, u32[]{:S(2)}) copy-start(f32[1,1024]{1,0:T(1,128)} %get-tuple-element.166) | copy-start | bytes 12292
  39.8 12.7 %copy-start.64 = (f32[1,1024]{1,0:T(1,128)S(1)}, f32[1,1024]{1,0:T(1,128)}, u32[]{:S(2)}) copy-start(f32[1,1024]{1,0:T(1,128)} %get-tuple-element.167) | copy-start | bytes 12292
  40.0 11.0 %collective-permute-start.4 = (bf16[1,2,4,16,1024]{4,3,2,1,0:T(8,128)(2,1)S(1)}, bf16[1,2,4,16,1024]{4,3,2,1,0:T(8,128)(2,1)S(1)}, u32[]{:S(2)}, u32[]{:S(2)}) collective-permute-start(bf16[1,2,4,16,1024]{4,3,2,1,0:T(8,128)(2,1)S(1)} %get-tuple-element.141), channel_id=1, source_target_pairs={{4,0},{8,4},{12,8},{5,1},{9,5},{13,9},{6,2},{10,6},{14,10},{7,3},{... | collective-permute-start | bytes 786440 | tf_op jit(solution)/shard_map/ppermute | solution.py:28
  41.3 9.7 %collective-permute-start.3 = (bf16[1,2,4,16,1024]{4,3,2,1,0:T(8,128)(2,1)S(1)}, bf16[1,2,4,16,1024]{4,3,2,1,0:T(8,128)(2,1)S(1)}, u32[]{:S(2)}, u32[]{:S(2)}) collective-permute-start(bf16[1,2,4,16,1024]{4,3,2,1,0:T(8,128)(2,1)S(1)} %get-tuple-element.142), channel_id=1, source_target_pairs={{0,4},{4,8},{8,12},{1,5},{5,9},{9,13},{2,6},{6,10},{10,14},{3,7},{... | collective-permute-start | bytes 786440 | tf_op jit(solution)/shard_map/ppermute | solution.py:27
  87.7 16.9 %copy-start = (bf16[1,4,4,16,1024]{4,3,2,1,0:T(8,128)(2,1)}, bf16[1,4,4,16,1024]{4,3,2,1,0:T(8,128)(2,1)S(1)}, u32[]{:S(2)}) copy-start(bf16[1,4,4,16,1024]{4,3,2,1,0:T(8,128)(2,1)S(1)} %get-tuple-element.268) | copy-start | bytes 1572868
  104.6 19.2 %copy-start.10 = (f32[1,4,4,16,1024]{4,3,2,1,0:T(8,128)S(1)}, f32[1,4,4,16,1024]{4,3,2,1,0:T(8,128)}, u32[]{:S(2)}) copy-start(f32[1,4,4,16,1024]{4,3,2,1,0:T(8,128)} %fusion.158) | copy-start | bytes 3145732
  117.4 91.9 %reduce-scatter.4.cloned.1.call-start = ((), (), s32[]{:S(2)}) async-start(), calls=%async_computation.3 | async-start | bytes 1310720 | tf_op jit(solution)/shard_map/reduce_scatter | solution.py:81
  117.4 11.3 %collective-permute-start.6 = (bf16[1,2,4,16,1024]{4,3,2,1,0:T(8,128)(2,1)S(1)}, bf16[1,2,4,16,1024]{4,3,2,1,0:T(8,128)(2,1)S(1)}, u32[]{:S(2)}, u32[]{:S(2)}) collective-permute-start(bf16[1,2,4,16,1024]{4,3,2,1,0:T(8,128)(2,1)S(1)} %get-tuple-element.139), channel_id=1, source_target_pairs={{4,0},{8,4},{12,8},{5,1},{9,5},{13,9},{6,2},{10,6},{14,10},{7,3},{... | collective-permute-start | bytes 786440 | tf_op jit(solution)/shard_map/ppermute | solution.py:28
  118.8 10.0 %collective-permute-start.5 = (bf16[1,2,4,16,1024]{4,3,2,1,0:T(8,128)(2,1)S(1)}, bf16[1,2,4,16,1024]{4,3,2,1,0:T(8,128)(2,1)S(1)}, u32[]{:S(2)}, u32[]{:S(2)}) collective-permute-start(bf16[1,2,4,16,1024]{4,3,2,1,0:T(8,128)(2,1)S(1)} %get-tuple-element.140), channel_id=1, source_target_pairs={{0,4},{4,8},{8,12},{1,5},{5,9},{9,13},{2,6},{6,10},{10,14},{3,7},{... | collective-permute-start | bytes 786440 | tf_op jit(solution)/shard_map/ppermute | solution.py:27
  128.7 108.6 %reduce-scatter.6.cloned.1.call-start = ((), (), s32[]{:S(2)}) async-start(), calls=%async_computation.5 | async-start | bytes 1310720 | tf_op jit(solution)/shard_map/reduce_scatter | solution.py:81
  165.0 145.9 %reduce-scatter.8.cloned.1.call-start = ((), (), s32[]{:S(2)}) async-start(), calls=%async_computation.6 | async-start | bytes 9437184 | tf_op jit(solution)/shard_map/reduce_scatter | solution.py:139
  181.3 27.9 %copy-start.9 = (bf16[1,4,4,16,512]{4,3,2,1,0:T(8,128)(2,1)S(1)}, bf16[1,4,4,16,512]{4,3,2,1,0:T(8,128)(2,1)}, u32[]{:S(2)}) copy-start(bf16[1,4,4,16,512]{4,3,2,1,0:T(8,128)(2,1)} %param.5) | copy-start | bytes 786436
  181.3 55.9 %copy-start.11 = (bf16[1,4,4,16,512]{4,3,2,1,0:T(8,128)(2,1)S(1)}, bf16[1,4,4,16,512]{4,3,2,1,0:T(8,128)(2,1)}, u32[]{:S(2)}) copy-start(bf16[1,4,4,16,512]{4,3,2,1,0:T(8,128)(2,1)} %param.9) | copy-start | bytes 786436
  (77 other events, 337.0 us)
Sparse Core Ops, SparseCore 0:
  12.5 34.7 all-gather.1
  117.5 62.7 all-reduce.3
  182.7 26.5 reduce-scatter.3
  211.4 25.8 reduce-scatter.5
  241.0 69.9 reduce-scatter.7
